TPU v7x, 128 devices: a whole 4x4x4 slice. The times are simulated.
128 devices in a mesh: prod: 32 (over x, y, core), pre: 4 (over z).
Axes of the slice: x: 4, y: 4, z: 4, core: 2. Of those that a mesh axis runs over, the one named last changes fastest.
Arguments:
- potentials: bfloat16 [512, 16, 512], P(('prod', 'pre')), may hold values from -6 to 6
- injected: float32 [512, 16, 512], P(('prod', 'pre')), may hold values from -6 to 6
- near_blocks: bfloat16 [512, 4, 512, 512], P('prod', 'pre'), may hold values from -0.125 to 0.125
- near_cols: int32 [512, 4], P('prod', 'pre'), may hold values from 0 to 511, as said below
- row_basis: bfloat16 [512, 16, 512], P('prod'), may hold values from -1.5 to 1.5
- col_basis: bfloat16 [512, 16, 512], P(('prod', 'pre')), may hold values from -0.25 to 0.25
- basis_ranks: int32 [512], P(('prod', 'pre')), may hold values from 1 to 16
- couplings: bfloat16 [512, 16, 8192], P('prod', None, 'pre'), may hold values from -0.0625 to 0.0625
- inverses: bfloat16 [512, 512, 512], P(('prod', 'pre')), may hold values from -0.25 to 0.25
Outputs:
- residual: float32 [512, 16, 512], P(('prod', 'pre'))
- corrected: float32 [512, 16, 512], P(('prod', 'pre'))
Inputs may be any that keep to these rules, and one draw needn't show every extreme that they name: near_cols[i, 0] = i; near_cols[i, 1] is i + 8 or i - 8; every other entry differs from i by 1 to 7.
All inputs are finite; a program needn't handle non-finite values.
Results may differ from a plain program's by a relative error of at most 0.012.
Values may be sent and summed in bfloat16 or wider, within the bound.
No kernel may reach another device: no remote copies, remote signals or barrier semaphores. Data moves between devices by JAX's collectives and lax.ppermute only.
A program may use at most 64 MiB of HBM per device.

v0:
```python
import jax
import jax.numpy as jnp
from jax import lax
from jax.sharding import PartitionSpec as P


def with_halo(block, sides, width):
    for axis, dim in sides:
        count = lax.axis_size(axis)
        forward = [(i, i + 1) for i in range(count - 1)]
        backward = [(target, source) for source, target in forward]
        low = lax.ppermute(
            lax.slice_in_dim(block, block.shape[dim] - width, None, axis=dim), axis, forward
        )
        high = lax.ppermute(lax.slice_in_dim(block, 0, width, axis=dim), axis, backward)
        block = jnp.concatenate([low, block, high], axis=dim)
    return block


def local(
    potentials,
    injected,
    near_blocks,
    near_cols,
    row_basis,
    col_basis,
    basis_ranks,
    couplings,
    inverses,
):
    rows_here = near_blocks.shape[0]
    owned_count = potentials.shape[0]
    scenarios = potentials.shape[1]
    rank_cap = col_basis.shape[1]
    band_width = rows_here // 2
    coeffs = lax.dot_general(
        potentials, col_basis, (((2,), (2,)), ((0,), (0,))), preferred_element_type=jnp.float32
    )
    levels = lax.broadcasted_iota(jnp.int32, (owned_count, rank_cap), 1)
    kept_levels = levels < basis_ranks[:, None]
    coeffs = jnp.where(kept_levels[:, None, :], coeffs, jnp.zeros_like(coeffs)).astype(jnp.bfloat16)
    coeffs = jnp.transpose(coeffs, (1, 0, 2)).reshape(scenarios, owned_count * rank_cap)
    column_coeffs = lax.all_gather(coeffs, "prod", axis=1, tiled=True)
    flat_couplings = couplings.reshape(rows_here * rank_cap, couplings.shape[2])
    weights = lax.dot_general(
        flat_couplings, column_coeffs, (((1,), (1,)), ((), ())), preferred_element_type=jnp.float32
    )
    weights = weights.reshape(rows_here, rank_cap, scenarios).astype(jnp.bfloat16)
    grouped = lax.all_gather(potentials, "pre", axis=0, tiled=True)
    banded = with_halo(grouped, (("prod", 0),), band_width)
    offset = lax.axis_index("prod") * rows_here - band_width
    local_index = near_cols - offset
    picked = banded[local_index]
    near_part = lax.dot_general(
        picked, near_blocks, (((1, 3), (1, 3)), ((0,), (0,))), preferred_element_type=jnp.float32
    )
    far_part = lax.dot_general(
        weights, row_basis, (((1,), (1,)), ((0,), (0,))), preferred_element_type=jnp.float32
    )
    partial_value = near_part + far_part
    summed = lax.psum_scatter(
        partial_value.astype(jnp.bfloat16), "pre", scatter_dimension=0, tiled=True
    ).astype(jnp.float32)
    residual = injected - summed
    halfway = residual.astype(jnp.bfloat16)
    corrected = lax.dot_general(
        halfway, inverses, (((2,), (2,)), ((0,), (0,))), preferred_element_type=jnp.float32
    )
    return (residual, corrected)


def solution(mesh):
    return jax.shard_map(
        local,
        mesh=mesh,
        in_specs=(
            P(("prod", "pre"), None, None),
            P(("prod", "pre"), None, None),
            P("prod", "pre", None, None),
            P("prod", "pre"),
            P("prod", None, None),
            P(("prod", "pre"), None, None),
            P(("prod", "pre")),
            P("prod", None, "pre"),
            P(("prod", "pre"), None, None),
        ),
        out_specs=(P(("prod", "pre"), None, None), P(("prod", "pre"), None, None)),
        check_vma=False,
    )
```

profile of v0, /device:TPU:0, one launch (start us, length us, event | category | flops | bytes accessed | tf_op | source)
XLA Modules:
  0.0 95.7 jit_solution(7576948068833928410)
XLA Ops:
  7.2 0.0 copy-start
  7.2 0.0 copy-start.2
  7.2 0.0 reduce-scatter.2.cloned.1.call-start
  7.2 13.9 %all_gather.6 = bf16[16,16,512]{2,1,0:T(8,128)(2,1)S(1)} all-gather(bf16[4,16,512]{2,1,0:T(8,128)(2,1)} %param.9), channel_id=1, replica_groups=mesh['prod'=32,'pre'=4] {'pre'}, dimensions={0}, use_global_device_ids=true | all-gather | bytes 327680 | tf_op jit(solution)/shard_map/all_gather | solution.py:49
  21.2 1.9 %collective-permute-start = (bf16[8,16,512]{2,1,0:T(8,128)(2,1)S(1)}, bf16[8,16,512]{2,1,0:T(8,128)(2,1)}, u32[]{:S(2)}, u32[]{:S(2)}) collective-permute-start(bf16[8,16,512]{2,1,0:T(8,128)(2,1)S(1)} %get-tuple-element.2), channel_id=1, source_target_pairs={{0,4},{4,8},{8,12},{12,16},{16,20},{20,24},{24,28},{28,32},{32,36}... | collective-permute-start | bytes 393224 | tf_op jit(solution)/shard_map/ppermute | solution.py:12
  23.1 1.3 %collective-permute-start.1 = (bf16[8,16,512]{2,1,0:T(8,128)(2,1)S(1)}, bf16[8,16,512]{2,1,0:T(8,128)(2,1)}, u32[]{:S(2)}, u32[]{:S(2)}) collective-permute-start(bf16[8,16,512]{2,1,0:T(8,128)(2,1)S(1)} %get-tuple-element.3), channel_id=1, source_target_pairs={{4,0},{8,4},{12,8},{16,12},{20,16},{24,20},{28,24},{32,28},{36,32}... | collective-permute-start | bytes 393224 | tf_op jit(solution)/shard_map/ppermute | solution.py:15
  24.4 0.7 iota_compare_fusion
  25.1 1.0 %fusion.9 = bf16[16,4,16]{2,0,1:T(8,128)(2,1)S(1)} fusion(bf16[4,16,512]{2,1,0:T(8,128)(2,1)} %param.9, bf16[4,16,512]{2,1,0:T(8,128)(2,1)} %param.14, pred[4,16]{1,0:T(4,128)(4,1)S(1)} %iota_compare_fusion), kind=kOutput, calls=%fused_computation.7 | convolution fusion | flops 1050624 | bytes 133184 | tf_op jit(solution)/shard_map/dot_general | solution.py:36
  26.2 0.1 reshape.35
  26.3 28.8 %all-gather = bf16[32,64,16]{1,2,0:T(8,128)(2,1)S(1)} all-gather(bf16[1,64,16]{1,2,0:T(8,128)(2,1)S(1)} %bitcast.29), channel_id=1, replica_groups=mesh['prod'=32,'pre'=4] {'prod'}, dimensions={0}, use_global_device_ids=true | all-gather | bytes 67584 | tf_op jit(solution)/shard_map/all_gather | solution.py:43
  55.1 0.2 reshape.48
  55.3 1.6 %fusion.10 = bf16[256,16]{0,1:T(8,128)(2,1)S(1)} fusion(bf16[2048,16]{0,1:T(8,128)(2,1)S(1)} %reshape.48, bf16[256,2048]{1,0:T(8,128)(2,1)} %bitcast.28), kind=kOutput, calls=%fused_computation.9 | convolution fusion | flops 16781312 | bytes 1122304 | tf_op jit(solution)/shard_map/dot_general | solution.py:45
  56.9 0.1 convert_element_type.29
  57.0 1.1 %fusion.11 = f32[16,16,512]{2,1,0:T(8,128)S(1)} fusion(bf16[16,16,512]{2,1,0:T(8,128)(2,1)} %param.13, bf16[16,16,16]{1,0,2:T(8,128)(2,1)S(1)} %convert_element_type.29), kind=kOutput, calls=%fused_computation.12 | convolution fusion | flops 4194304 | bytes 794624 | tf_op jit(solution)/shard_map/dot_general | solution.py:57
  58.2 0.7 fusion.15
  58.9 0.0 collective-permute-done
  58.9 0.0 collective-permute-done.1
  58.9 1.0 %pad_maximum_fusion = bf16[32,16,512]{2,1,0:T(8,128)(2,1)S(1)} fusion(bf16[8,16,512]{2,1,0:T(8,128)(2,1)} %collective-permute-done.1, bf16[16,16,512]{2,1,0:T(8,128)(2,1)S(1)} %all_gather.6, bf16[8,16,512]{2,1,0:T(8,128)(2,1)} %collective-permute-done), kind=kLoop, calls=%fused_computation.10 | loop fusion | flops 524288 | bytes 1048576 | tf_op jit(solution)/shard_map/concatenate | solution.py:16
  59.9 0.6 gather_fusion
  60.5 6.4 %fusion.5 = bf16[16,16,512]{2,1,0:T(8,128)(2,1)} fusion(f32[16,16,512]{2,1,0:T(8,128)S(1)} %fusion.11, bf16[16,16,512]{2,1,0:T(8,128)(2,1)S(1)} %gather_fusion, bf16[16,1,512,512]{3,2,1,0:T(8,128)(2,1)} %param.11), kind=kOutput, calls=%fused_computation.4 | convolution fusion | flops 134479872 | bytes 9437184 | tf_op jit(solution)/shard_map/dot_general | solution.py:54
  66.9 0.0 reduce-scatter.2.cloned.1.call-update
  66.9 19.8 %reduce-scatter.2.cloned.1.call-done = bf16[4,16,512]{2,1,0:T(8,128)(2,1)} async-done(((bf16[16,16,512]{2,1,0:T(8,128)(2,1)}), bf16[4,16,512]{2,1,0:T(8,128)(2,1)}) %reduce-scatter.2.cloned.1.call-update) | async-done | bytes 65552 | tf_op jit(solution)/shard_map/reduce_scatter | solution.py:61
  86.7 0.0 copy-done.2
  86.7 0.9 convert_subtract_fusion
  87.5 0.0 copy-done
  87.5 0.0 copy-start.1
  87.6 1.3 %fusion.13 = f32[4,16,512]{2,1,0:T(8,128)} fusion(bf16[4,512,512]{2,1,0:T(8,128)(2,1)S(1)} %copy-done, f32[4,16,512]{2,1,0:T(8,128)S(1)} %convert_subtract_fusion), kind=kOutput, calls=%fused_computation.14 | convolution fusion | flops 33587200 | bytes 2359296 | tf_op jit(solution)/shard_map/dot_general | solution.py:66
  88.9 0.0 copy-done.1
  (4 shorter events, 0.1 us)
Async XLA Ops:
  7.2 80.4 %copy-start = (bf16[4,512,512]{2,1,0:T(8,128)(2,1)S(1)}, bf16[4,512,512]{2,1,0:T(8,128)(2,1)}, u32[]{:S(2)}) copy-start(bf16[4,512,512]{2,1,0:T(8,128)(2,1)} %param.17) | copy-start | bytes 6291460
  7.2 79.5 %copy-start.2 = (f32[4,16,512]{2,1,0:T(8,128)S(1)}, f32[4,16,512]{2,1,0:T(8,128)}, u32[]{:S(2)}) copy-start(f32[4,16,512]{2,1,0:T(8,128)} %param.10) | copy-start | bytes 393220
  7.2 79.5 %reduce-scatter.2.cloned.1.call-start = ((), (), s32[]{:S(2)}) async-start(), calls=%async_computation.1 | async-start | bytes 327680 | tf_op jit(solution)/shard_map/reduce_scatter | solution.py:61
  21.2 37.7 %collective-permute-start = (bf16[8,16,512]{2,1,0:T(8,128)(2,1)S(1)}, bf16[8,16,512]{2,1,0:T(8,128)(2,1)}, u32[]{:S(2)}, u32[]{:S(2)}) collective-permute-start(bf16[8,16,512]{2,1,0:T(8,128)(2,1)S(1)} %get-tuple-element.2), channel_id=1, source_target_pairs={{0,4},{4,8},{8,12},{12,16},{16,20},{20,24},{24,28},{28,32},{32,36}... | collective-permute-start | bytes 393224 | tf_op jit(solution)/shard_map/ppermute | solution.py:12
  23.1 35.8 %collective-permute-start.1 = (bf16[8,16,512]{2,1,0:T(8,128)(2,1)S(1)}, bf16[8,16,512]{2,1,0:T(8,128)(2,1)}, u32[]{:S(2)}, u32[]{:S(2)}) collective-permute-start(bf16[8,16,512]{2,1,0:T(8,128)(2,1)S(1)} %get-tuple-element.3), channel_id=1, source_target_pairs={{4,0},{8,4},{12,8},{16,12},{20,16},{24,20},{28,24},{32,28},{36,32}... | collective-permute-start | bytes 393224 | tf_op jit(solution)/shard_map/ppermute | solution.py:15
  87.5 1.3 %copy-start.1 = (f32[4,16,512]{2,1,0:T(8,128)}, f32[4,16,512]{2,1,0:T(8,128)S(1)}, u32[]{:S(2)}) copy-start(f32[4,16,512]{2,1,0:T(8,128)S(1)} %convert_subtract_fusion) | copy-start | bytes 393220
Sparse Core Ops, SparseCore 0:
  67.0 19.6 reduce-scatter.1
where the time goes:
time: 96.1 us; the launch traced here: 95.7 us
  blocking collectives  42.7 us (44%)
  waiting for transfers between devices  19.8 us (21%)
  between operations  14.1 us (15%)
  matrix products  11.4 us (12%)
  other arithmetic  3.29 us (3%)
  starting transfers between devices  3.27 us (3%)
  local copies, waits for them, and re-layouts  1.04 us (1%)
    all_gather x1, blocking collectives, local(): column_coeffs = lax.all_gather(coeffs, 'prod', axis=1, tiled=True)  28.8 us
    reduce_scatter x1, waiting for transfers between devices, local(): lax.psum_scatter(partial_value.astype(jnp.bfloat16), 'pre', scatter_dimen...  19.8 us
    all_gather x1, blocking collectives, local(): grouped = lax.all_gather(potentials, 'pre', axis=0, tiled=True)  13.9 us
    dot_general x1, matrix products, local(): lax.dot_general(picked, near_blocks, (((1, 3), (1, 3)), ((0,), (0,))), pr...  6.38 us
    ppermute x1, starting transfers between devices, with_halo(): lax.ppermute(lax.slice_in_dim(block, block.shape[dim] - width, None, axis...  1.95 us
  transfers between devices with their start and end apart: 3, of which 1 were waited for; matrix products, arithmetic and copies ran while one was open for 6% of the time, Pallas kernels for 0%

commit v1 on v0

v1 whole, which is shorter than its diff:
```python
import functools

import jax
import jax.numpy as jnp
from jax import lax
from jax.experimental import pallas as pl
from jax.experimental.pallas import tpu as pltpu
from jax.sharding import PartitionSpec as P

AXES = ("prod", "pre")
GRAY = (0, 1, 3, 2)
NT = (((1,), (1,)), ((), ()))
F32 = jnp.float32
BF16 = jnp.bfloat16


def pairs(rule):
    table = []
    for p in range(32):
        for a in range(4):
            q, b = rule(p, a)
            table.append((p * 4 + a, q * 4 + b))
    return table


def first_mask(p):
    return 1 if p % 2 == 0 else 3


CORE_SWAP = pairs(lambda p, a: (p ^ 1, a))
Y_SWAPS = tuple(pairs(lambda p, a, m=m: (p ^ (2 * m), a)) for m in (1, 3))
X_SWAPS = tuple(pairs(lambda p, a, m=m: (p ^ (8 * m), a)) for m in (1, 3))
Z_FIRST = pairs(lambda p, a: (p, a ^ first_mask(p)))
Z_SECOND = pairs(lambda p, a: (p, a ^ first_mask(p) ^ 2))
OTHER_CHIP = pairs(lambda p, a: ((p + 1) % 32 if p % 2 else (p - 1) % 32, a))


def send(x, table):
    return lax.ppermute(x, AXES, table)


def place():
    p = lax.axis_index("prod")
    a = lax.axis_index("pre")
    core = p & 1
    first = 1 + 2 * core
    second = 3 - 2 * core
    return p, a, core, first, second


def coeff_kernel(pot_ref, basis_ref, ranks_ref, out_ref):
    p = lax.axis_index("prod")
    pot = pot_ref[...].reshape(64, 512)
    basis = basis_ref[...].reshape(64, 512)
    both = jnp.concatenate([basis, basis], axis=0)
    full = lax.dot_general(pot, both, NT, preferred_element_type=F32)
    lane = lax.broadcasted_iota(jnp.int32, (16, 128), 1)
    here = (lane >> 6) == (p & 1)
    total = jnp.zeros((16, 128), F32)
    for j in range(4):
        keep = here & (((lane >> 4) & 3) == j) & ((lane & 15) < ranks_ref[j])
        total = total + jnp.where(keep, full[j * 16:(j + 1) * 16, :], 0.0)
    out_ref[...] = total.astype(BF16)


def far_kernel(near_half_ref, far_half_ref, couplings_ref, row_ref, out_ref, gathered):
    p = lax.axis_index("prod")
    x = p >> 3
    y = (p >> 1) & 3
    for r in range(16):
        chip = (x ^ GRAY[r // 4]) * 4 + (y ^ GRAY[r % 4])
        piece = near_half_ref[r] if r < 8 else far_half_ref[r - 8]
        gathered[:, pl.ds(pl.multiple_of(chip * 128, 128), 128)] = piece
    weights = lax.dot_general(gathered[...], couplings_ref[...], NT, preferred_element_type=F32)
    tall = jnp.concatenate([weights] * 16, axis=0)
    row = lax.broadcasted_iota(jnp.int32, (256, 256), 0) >> 4
    col = lax.broadcasted_iota(jnp.int32, (256, 256), 1) >> 4
    spread = jnp.where(row == col, tall, 0.0).astype(BF16)
    out_ref[...] = jnp.dot(spread, row_ref[...], preferred_element_type=F32)


def select_kernel(own_ref, other_ref, group_ref, chip_ref, out_ref):
    p, a, core, first, second = place()
    for z in range(4):
        d = a ^ z
        slot = jnp.where(d == 0, 0, jnp.where(d == first, 1, jnp.where(d == second, 2, 3)))
        at = pl.multiple_of((slot & 1) * 4, 4)
        piece = jnp.where(slot < 2, own_ref[pl.ds(at, 4)], other_ref[pl.ds(at, 4)])
        group_ref[z * 4:(z + 1) * 4] = piece
        to_chip = (z < 2) == (core == 1) if False else ((z >> 1) ^ core) == 1

        @pl.when(to_chip)
        def _():
            chip_ref[(z & 1) * 4:(z & 1) * 4 + 4] = piece

        @pl.when(jnp.logical_not(to_chip))
        def _():
            out_ref[(z & 1) * 4:(z & 1) * 4 + 4] = piece


def near_kernel(keep, cols_ref, group_ref, chip_ref, outer_ref, near_ref, far_ref, out_ref):
    p, a, core, first, second = place()
    base = p * 16
    for half in range(2):
        if keep:
            piece = a if half == 0 else a ^ second
        else:
            piece = a ^ first if half == 0 else a ^ 2
        for j in range(4):
            i = piece * 4 + j
            c = cols_ref[i] - base
            below = c < 0
            above = c >= 16
            halo = jnp.clip(jnp.where(below, c + 8, c - 16), 0, 7)
            from_chip = (below & (core == 1)) | (above & (core == 0))
            inside = jnp.logical_not(below | above)
            picked = jnp.where(from_chip, chip_ref[halo], outer_ref[halo])
            picked = jnp.where(inside, group_ref[jnp.clip(c, 0, 15)], picked)
            block = lax.dot_general(picked, near_ref[i], NT, preferred_element_type=F32)
            rows = pl.ds(pl.multiple_of(i * 16, 16), 16)
            out_ref[half * 4 + j] = (block + far_ref[rows, :]).astype(out_ref.dtype)


def fold_kernel(kept_ref, got_ref, out_ref):
    out_ref[...] = (kept_ref[4:8] + got_ref[4:8].astype(F32)).astype(BF16)


def final_kernel(kept_ref, got_ref, last_ref, injected_ref, inverse_ref, residual_ref, corrected_ref):
    for j in range(4):
        total = kept_ref[j] + got_ref[j].astype(F32) + last_ref[j].astype(F32)
        residual = injected_ref[j] - total
        residual_ref[j] = residual
        corrected_ref[j] = lax.dot_general(
            residual.astype(BF16), inverse_ref[j], NT, preferred_element_type=F32
        )


VMEM = pl.BlockSpec(memory_space=pltpu.VMEM)
SMEM = pl.BlockSpec(memory_space=pltpu.SMEM)


def call(kernel, out_shape, in_specs, name, scratch=(), flops=0, moved=0):
    many = isinstance(out_shape, (list, tuple))
    return pl.pallas_call(
        kernel,
        out_shape=out_shape,
        in_specs=in_specs,
        out_specs=[VMEM] * len(out_shape) if many else VMEM,
        scratch_shapes=list(scratch),
        compiler_params=pltpu.CompilerParams(vmem_limit_bytes=24 * 2**20),
        cost_estimate=pl.CostEstimate(flops=flops, bytes_accessed=moved, transcendentals=0),
        name=name,
    )


def shape(dims, dtype):
    return jax.ShapeDtypeStruct(dims, dtype)


def local(
    potentials,
    injected,
    near_blocks,
    near_cols,
    row_basis,
    col_basis,
    basis_ranks,
    couplings,
    inverses,
):
    first_z = send(potentials, Z_FIRST)
    coeffs = call(coeff_kernel, shape((16, 128), BF16), [VMEM, VMEM, SMEM], "coeffs", moved=2**17)(
        potentials, col_basis, basis_ranks
    )
    gathered = (coeffs + send(coeffs, CORE_SWAP))[None]
    for table in (Y_SWAPS[0], Y_SWAPS[1], X_SWAPS[0]):
        gathered = jnp.concatenate([gathered, send(gathered, table)], axis=0)
    others = send(gathered, X_SWAPS[1])
    own_pair = jnp.concatenate([potentials, first_z], axis=0)
    second_z = send(own_pair, Z_SECOND)
    group, to_chip, to_outer = call(
        select_kernel,
        [shape((16, 16, 512), BF16), shape((8, 16, 512), BF16), shape((8, 16, 512), BF16)],
        [VMEM, VMEM], "select", moved=2**19,
    )(own_pair, second_z)
    outer = send(to_outer, OTHER_CHIP)
    chip = send(to_chip, CORE_SWAP)
    far = call(
        far_kernel, shape((256, 512), F32), [VMEM] * 4, "far",
        scratch=[pltpu.VMEM((16, 2048), BF16)], moved=2**21, flops=2**26,
    )(gathered, others, couplings.reshape(256, 2048), row_basis.reshape(256, 512))
    blocks = near_blocks.reshape(16, 512, 512)
    cols = near_cols.reshape(16)
    near_specs = [SMEM] + [VMEM] * 5
    sent = call(
        functools.partial(near_kernel, False), shape((8, 16, 512), BF16), near_specs, "near_sent",
        moved=2**22, flops=2**26,
    )(cols, group, chip, outer, blocks, far)
    got = send(sent, Z_FIRST)
    kept = call(
        functools.partial(near_kernel, True), shape((8, 16, 512), F32), near_specs, "near_kept",
        moved=2**22, flops=2**26,
    )(cols, group, chip, outer, blocks, far)
    folded = call(fold_kernel, shape((4, 16, 512), BF16), [VMEM] * 2, "fold", moved=2**18)(kept, got)
    last = send(folded, Z_SECOND)
    return call(
        final_kernel, [shape((4, 16, 512), F32), shape((4, 16, 512), F32)], [VMEM] * 5, "final",
        moved=2**21, flops=2**25,
    )(kept, got, last, injected, inverses)


def solution(mesh):
    return jax.shard_map(
        local,
        mesh=mesh,
        in_specs=(
            P(("prod", "pre"), None, None),
            P(("prod", "pre"), None, None),
            P("prod", "pre", None, None),
            P("prod", "pre"),
            P("prod", None, None),
            P(("prod", "pre"), None, None),
            P(("prod", "pre")),
            P("prod", None, "pre"),
            P(("prod", "pre"), None, None),
        ),
        out_specs=(P(("prod", "pre"), None, None), P(("prod", "pre"), None, None)),
        check_vma=False,
    )
```

time: 96.1 us -> 48 us (0.50)
  blocking collectives: 42.7 us -> 0 us
  starting transfers between devices: 3.27 us -> 19 us
  between operations: 14.1 us -> 0.73 us
  matrix products: 11.4 us -> 0 us
  local copies, waits for them, and re-layouts: 1.04 us -> 8.55 us
  waiting for transfers between devices: 19.8 us -> 13 us
  Pallas kernels: 0 us -> 6.29 us
  other arithmetic: 3.29 us -> 0.02 us
    all_gather x2 -> x0, blocking collectives: 42.7 us -> none  [the longest x1 28.8 us: local(): column_coeffs = lax.all_gather(coeffs, 'prod', axis=1, tiled=True)]
    reduce_scatter x1 -> x0, waiting for transfers between devices: 19.8 us -> none  [local(): lax.psum_scatter(partial_value.astype(jnp.bfloat16), 'pre', scatter_dimen...]
    ppermute x2 -> x11, starting transfers between devices: 3.23 us -> 19 us  [send(): return lax.ppermute(x, AXES, table)]
    ppermute x2 -> x11, waiting for transfers between devices: 0.01 us -> 13 us  [send(): return lax.ppermute(x, AXES, table)]
    dot_general x5 -> x0, matrix products: 11.4 us -> none  [the longest x1 6.38 us: local(): lax.dot_general(picked, near_blocks, (((1, 3), (1, 3)), ((0,), (0,))), pr...]
    unnamed x7 -> x19, local copies, waits for them, and re-layouts: 0.2 us -> 8.54 us
    pallas_call x0 -> x7, Pallas kernels: none -> 6.29 us  [the longest x1 1.74 us: local(): call(functools.partial(near_kernel, False), shape((8, 16, 512), BF16), ne...]
    concatenate x1 -> x3, other arithmetic: 1.03 us -> 0.01 us  [local(): gathered = jnp.concatenate([gathered, send(gathered, table)], axis=0)]
  transfers between devices with their start and end apart: 3 -> 11, of which waited for: 1 -> 5; matrix products, arithmetic and copies ran while one was open for 6% -> 0% of each run, Pallas kernels for 0% -> 5%
where the time goes in v1:
time: 48 us; the launch traced here: 47.6 us
  starting transfers between devices  19 us (40%)
  waiting for transfers between devices  13 us (27%)
  local copies, waits for them, and re-layouts  8.55 us (18%)
  Pallas kernels  6.29 us (13%)
  between operations  0.73 us (2%)
    ppermute x11, starting transfers between devices, send(): return lax.ppermute(x, AXES, table)  19 us
    ppermute x11, waiting for transfers between devices, send(): return lax.ppermute(x, AXES, table)  13 us
    unnamed x19, local copies, waits for them, and re-layouts  8.54 us
    pallas_call x1, Pallas kernels, local(): call(functools.partial(near_kernel, False), shape((8, 16, 512), BF16), ne...  1.74 us
    pallas_call x1, Pallas kernels, local(): call(functools.partial(near_kernel, True), shape((8, 16, 512), F32), near...  1.74 us
    pallas_call x1, Pallas kernels, local(): call(final_kernel, [shape((4, 16, 512), F32), shape((4, 16, 512), F32)],...  1.32 us
  transfers between devices with their start and end apart: 11, of which 5 were waited for; matrix products, arithmetic and copies ran while one was open for 0% of the time, Pallas kernels for 5%

profile of v1, /device:TPU:0, one launch (start us, length us, event | category | flops | bytes accessed | tf_op | source)
XLA Modules:
  0.0 47.6 jit_solution(7764538917307951009)
XLA Ops:
  0.6 0.0 copy-start.3
  0.6 0.8 %copy-done.3 = bf16[4,16,512]{2,1,0:T(8,128)(2,1)S(1)} copy-done((bf16[4,16,512]{2,1,0:T(8,128)(2,1)S(1)}, bf16[4,16,512]{2,1,0:T(8,128)(2,1)}, u32[]{:S(2)}) %copy-start.3) | copy-done | bytes 65560
  1.5 0.0 copy-start.6
  1.5 0.8 %copy-done.6 = bf16[4,16,512]{2,1,0:T(8,128)(2,1)S(1)} copy-done((bf16[4,16,512]{2,1,0:T(8,128)(2,1)S(1)}, bf16[4,16,512]{2,1,0:T(8,128)(2,1)}, u32[]{:S(2)}) %copy-start.6) | copy-done | bytes 65560
  2.3 0.0 copy-start.8
  2.3 0.7 %copy-done.8 = s32[4]{0:T(128)S(1)} copy-done((s32[4]{0:T(128)S(1)}, s32[4]{0:T(128)}, u32[]{:S(2)}) %copy-start.8) | copy-done | bytes 40
  3.0 0.7 %coeffs.1 = bf16[16,128]{1,0:T(8,128)(2,1)S(1)} custom-call(bf16[4,16,512]{2,1,0:T(8,128)(2,1)S(1)} %copy-done.3, bf16[4,16,512]{2,1,0:T(8,128)(2,1)S(1)} %copy-done.6, s32[4]{0:T(128)S(1)} %copy-done.8), custom_call_target="tpu_custom_call" | custom-call | bytes 131072 | tf_op jit(solution)/shard_map/coeffs/pallas_call | solution.py:172
  3.7 0.1 collective-permute-start.4
  3.8 2.1 %collective-permute-start = (bf16[4,16,512]{2,1,0:T(8,128)(2,1)S(1)}, bf16[4,16,512]{2,1,0:T(8,128)(2,1)S(1)}, u32[]{:S(2)}, u32[]{:S(2)}) collective-permute-start(bf16[4,16,512]{2,1,0:T(8,128)(2,1)S(1)} %copy-done.3), channel_id=1, source_target_pairs={{0,1},{1,0},{2,3},{3,2},{4,7},{5,6},{6,5},{7,4},{8,9},{9,8},{10,11... | collective-permute-start | bytes 196616 | tf_op jit(solution)/shard_map/ppermute | solution.py:39
  5.9 0.0 collective-permute-done.4
  5.9 1.6 %collective-permute-start.5 = (bf16[1,16,128]{2,1,0:T(8,128)(2,1)S(1)}, bf16[1,16,128]{2,1,0:T(8,128)(2,1)S(1)}, u32[]{:S(2)}, u32[]{:S(2)}) collective-permute-start(bf16[1,16,128]{2,1,0:T(8,128)(2,1)S(1)} %add_bitcast_fusion), channel_id=1, source_target_pairs={{0,8},{1,9},{2,10},{3,11},{4,12},{5,13},{6,14},{7,15},{8,0},{9,1},... | collective-permute-start | bytes 12296 | tf_op jit(solution)/shard_map/ppermute | solution.py:39
  7.5 2.0 %collective-permute-done.5 = bf16[1,16,128]{2,1,0:T(8,128)(2,1)S(1)} collective-permute-done((bf16[1,16,128]{2,1,0:T(8,128)(2,1)S(1)}, bf16[1,16,128]{2,1,0:T(8,128)(2,1)S(1)}, u32[]{:S(2)}, u32[]{:S(2)}) %collective-permute-start.5) | collective-permute-done | bytes 4128 | tf_op jit(solution)/shard_map/ppermute | solution.py:39
  9.5 3.0 %collective-permute-start.6 = (bf16[2,16,128]{2,1,0:T(8,128)(2,1)S(1)}, bf16[2,16,128]{2,1,0:T(8,128)(2,1)S(1)}, u32[]{:S(2)}, u32[]{:S(2)}) collective-permute-start(bf16[2,16,128]{2,1,0:T(8,128)(2,1)S(1)} %pad_maximum_fusion.2), channel_id=1, source_target_pairs={{0,24},{1,25},{2,26},{3,27},{4,28},{5,29},{6,30},{7,31},{8,16},{9,... | collective-permute-start | bytes 24584 | tf_op jit(solution)/shard_map/ppermute | solution.py:39
  12.5 0.0 collective-permute-done
  12.5 3.3 %collective-permute-start.1 = (bf16[8,16,512]{2,1,0:T(8,128)(2,1)S(1)}, bf16[8,16,512]{2,1,0:T(8,128)(2,1)S(1)}, u32[]{:S(2)}, u32[]{:S(2)}) collective-permute-start(bf16[8,16,512]{2,1,0:T(8,128)(2,1)S(1)} %constant_dynamic-update-slice_fusion.own_ref), channel_id=1, source_target_pairs={{0,3},{1,2},{2,1},{3,0},{4,5},{5,4},{6,7},{7,6},{8,11},{9,10},{10,... | collective-permute-start | bytes 393224 | tf_op jit(solution)/shard_map/ppermute | solution.py:39
  15.8 0.0 collective-permute-done.6
  15.8 1.6 %collective-permute-start.7 = (bf16[4,16,128]{2,1,0:T(8,128)(2,1)S(1)}, bf16[4,16,128]{2,1,0:T(8,128)(2,1)S(1)}, u32[]{:S(2)}, u32[]{:S(2)}) collective-permute-start(bf16[4,16,128]{2,1,0:T(8,128)(2,1)S(1)} %pad_maximum_fusion.1), channel_id=1, source_target_pairs={{0,32},{1,33},{2,34},{3,35},{4,36},{5,37},{6,38},{7,39},{8,40},{9,... | collective-permute-start | bytes 49160 | tf_op jit(solution)/shard_map/ppermute | solution.py:39
  17.4 1.4 %collective-permute-done.1.other_ref = bf16[8,16,512]{2,1,0:T(8,128)(2,1)S(1)} collective-permute-done((bf16[8,16,512]{2,1,0:T(8,128)(2,1)S(1)}, bf16[8,16,512]{2,1,0:T(8,128)(2,1)S(1)}, u32[]{:S(2)}, u32[]{:S(2)}) %collective-permute-start.1) | collective-permute-done | bytes 131104 | tf_op jit(solution)/shard_map/ppermute | solution.py:39
  18.8 0.1 select.1
  18.9 0.1 collective-permute-start.2
  18.9 2.5 %collective-permute-start.3 = (bf16[8,16,512]{2,1,0:T(8,128)(2,1)S(1)}, bf16[8,16,512]{2,1,0:T(8,128)(2,1)S(1)}, u32[]{:S(2)}, u32[]{:S(2)}) collective-permute-start(bf16[8,16,512]{2,1,0:T(8,128)(2,1)S(1)} %get-tuple-element.7), channel_id=1, source_target_pairs={{0,124},{1,125},{2,126},{3,127},{4,8},{5,9},{6,10},{7,11},{8,4},{9... | collective-permute-start | bytes 393224 | tf_op jit(solution)/shard_map/ppermute | solution.py:39
  21.5 0.0 collective-permute-done.7
  21.5 1.0 %collective-permute-start.8 = (bf16[8,16,128]{2,1,0:T(8,128)(2,1)S(1)}, bf16[8,16,128]{2,1,0:T(8,128)(2,1)S(1)}, u32[]{:S(2)}, u32[]{:S(2)}) collective-permute-start(bf16[8,16,128]{2,1,0:T(8,128)(2,1)S(1)} %pad_maximum_fusion.near_half_ref), channel_id=1, source_target_pairs={{0,96},{1,97},{2,98},{3,99},{4,100},{5,101},{6,102},{7,103},{8,104... | collective-permute-start | bytes 98312 | tf_op jit(solution)/shard_map/ppermute | solution.py:39
  22.4 4.2 %collective-permute-done.8.far_half_ref = bf16[8,16,128]{2,1,0:T(8,128)(2,1)S(1)} collective-permute-done((bf16[8,16,128]{2,1,0:T(8,128)(2,1)S(1)}, bf16[8,16,128]{2,1,0:T(8,128)(2,1)S(1)}, u32[]{:S(2)}, u32[]{:S(2)}) %collective-permute-start.8) | collective-permute-done | bytes 32800 | tf_op jit(solution)/shard_map/ppermute | solution.py:39
  26.7 0.0 copy-start.2
  26.7 1.2 %copy-done.2 = bf16[16,16,2048]{2,1,0:T(8,128)(2,1)S(1)} copy-done((bf16[16,16,2048]{2,1,0:T(8,128)(2,1)S(1)}, bf16[16,16,2048]{2,1,0:T(8,128)(2,1)}, u32[]{:S(2)}) %copy-start.2) | copy-done | bytes 1048600
  27.9 0.0 copy-start.4
  27.9 0.9 %copy-done.4 = bf16[16,16,512]{2,1,0:T(8,128)(2,1)S(1)} copy-done((bf16[16,16,512]{2,1,0:T(8,128)(2,1)S(1)}, bf16[16,16,512]{2,1,0:T(8,128)(2,1)}, u32[]{:S(2)}) %copy-start.4) | copy-done | bytes 262168
  28.9 0.7 %far.1.far_ref = f32[256,512]{1,0:T(8,128)S(1)} custom-call(bf16[8,16,128]{2,1,0:T(8,128)(2,1)S(1)} %pad_maximum_fusion.near_half_ref, bf16[8,16,128]{2,1,0:T(8,128)(2,1)S(1)} %collective-permute-done.8.far_half_ref, bf16[256,2048]{1,0:T(8,128)(2,1)S(1)} %bitcast.8, bf16[256,512]{1,0:T(8,128)(2,1)S(1)} %bitcast.9), custom_call_target="tpu_custom_call" | custom-call | flops 67108864 | bytes 2097152 | tf_op jit(solution)/shard_map/far/pallas_call | solution.py:188
  29.6 0.0 collective-permute-done.2.chip_ref
  29.6 0.0 collective-permute-done.3.outer_ref
  29.6 0.0 copy-start
  29.6 3.4 %copy-done = bf16[16,1,512,512]{3,2,1,0:T(8,128)(2,1)S(1)} copy-done((bf16[16,1,512,512]{3,2,1,0:T(8,128)(2,1)S(1)}, bf16[16,1,512,512]{3,2,1,0:T(8,128)(2,1)}, u32[]{:S(2)}) %copy-start) | copy-done | bytes 8388632
  33.0 0.0 copy-start.7
  33.0 0.7 %copy-done.7 = s32[16,1]{0,1:T(1,128)S(1)} copy-done((s32[16,1]{0,1:T(1,128)S(1)}, s32[16,1]{0,1:T(1,128)}, u32[]{:S(2)}) %copy-start.7) | copy-done | bytes 88
  33.6 0.0 copy-start.1
  33.6 0.0 copy-start.5
  33.6 1.7 %near_sent.1 = bf16[8,16,512]{2,1,0:T(8,128)(2,1)S(1)} custom-call(s32[16]{0:T(128)S(1)} %bitcast.10, bf16[16,16,512]{2,1,0:T(8,128)(2,1)S(1)} %get-tuple-element.5.group_ref, bf16[8,16,512]{2,1,0:T(8,128)(2,1)S(1)} %collective-permute-done.2.chip_ref, bf16[8,16,512]{2,1,0:T(8,128)(2,1)S(1)} %collective-permute-done.3.outer_ref, ...), custom_call_target="tpu_custom_call" | custom-call | flops 67108864 | bytes 4194304 | tf_op jit(solution)/shard_map/near_sent/pallas_call | solution.py:195
  35.4 0.3 collective-permute-start.9
  35.7 1.7 %near_kept.1.kept_ref = f32[8,16,512]{2,1,0:T(8,128)S(1)} custom-call(s32[16]{0:T(128)S(1)} %bitcast.11, bf16[16,16,512]{2,1,0:T(8,128)(2,1)S(1)} %get-tuple-element.5.group_ref, bf16[8,16,512]{2,1,0:T(8,128)(2,1)S(1)} %collective-permute-done.2.chip_ref, bf16[8,16,512]{2,1,0:T(8,128)(2,1)S(1)} %collective-permute-done.3.outer_ref, ...), custom_call_target="tpu_custom_call" | custom-call | flops 67108864 | bytes 4194304 | tf_op jit(solution)/shard_map/near_kept/pallas_call | solution.py:200
  37.4 3.1 %collective-permute-done.9.got_ref = bf16[8,16,512]{2,1,0:T(8,128)(2,1)S(1)} collective-permute-done((bf16[8,16,512]{2,1,0:T(8,128)(2,1)S(1)}, bf16[8,16,512]{2,1,0:T(8,128)(2,1)S(1)}, u32[]{:S(2)}, u32[]{:S(2)}) %collective-permute-start.9) | collective-permute-done | bytes 131104 | tf_op jit(solution)/shard_map/ppermute | solution.py:39
  40.6 3.5 %collective-permute-start.10 = (bf16[4,16,512]{2,1,0:T(8,128)(2,1)S(1)}, bf16[4,16,512]{2,1,0:T(8,128)(2,1)S(1)}, u32[]{:S(2)}, u32[]{:S(2)}) collective-permute-start(bf16[4,16,512]{2,1,0:T(8,128)(2,1)S(1)} %fold.1), channel_id=1, source_target_pairs={{0,3},{1,2},{2,1},{3,0},{4,5},{5,4},{6,7},{7,6},{8,11},{9,10},{10,... | collective-permute-start | bytes 196616 | tf_op jit(solution)/shard_map/ppermute | solution.py:39
  44.1 2.2 %collective-permute-done.10.last_ref = bf16[4,16,512]{2,1,0:T(8,128)(2,1)S(1)} collective-permute-done((bf16[4,16,512]{2,1,0:T(8,128)(2,1)S(1)}, bf16[4,16,512]{2,1,0:T(8,128)(2,1)S(1)}, u32[]{:S(2)}, u32[]{:S(2)}) %collective-permute-start.10) | collective-permute-done | bytes 65568 | tf_op jit(solution)/shard_map/ppermute | solution.py:39
  46.3 0.0 copy-done.1
  46.3 0.0 copy-done.5
  46.3 1.3 %final.1 = (f32[4,16,512]{2,1,0:T(8,128)}, f32[4,16,512]{2,1,0:T(8,128)}) custom-call(f32[8,16,512]{2,1,0:T(8,128)S(1)} %near_kept.1.kept_ref, bf16[8,16,512]{2,1,0:T(8,128)(2,1)S(1)} %collective-permute-done.9.got_ref, bf16[4,16,512]{2,1,0:T(8,128)(2,1)S(1)} %collective-permute-done.10.last_ref, f32[4,16,512]{2,1,0:T(8,128)S(1)} %copy-done.5, ...), custom_call_target="tpu_custom_call" | custom-call | flops 33554432 | bytes 2097152 | tf_op jit(solution)/shard_map/final/pallas_call | solution.py:206
  (7 shorter events, 0.0 us)
Async XLA Ops:
  0.6 0.8 %copy-start.3 = (bf16[4,16,512]{2,1,0:T(8,128)(2,1)S(1)}, bf16[4,16,512]{2,1,0:T(8,128)(2,1)}, u32[]{:S(2)}) copy-start(bf16[4,16,512]{2,1,0:T(8,128)(2,1)} %pot_ref.1) | copy-start | bytes 196612
  1.5 0.8 %copy-start.6 = (bf16[4,16,512]{2,1,0:T(8,128)(2,1)S(1)}, bf16[4,16,512]{2,1,0:T(8,128)(2,1)}, u32[]{:S(2)}) copy-start(bf16[4,16,512]{2,1,0:T(8,128)(2,1)} %basis_ref.1) | copy-start | bytes 196612
  2.3 0.7 %copy-start.8 = (s32[4]{0:T(128)S(1)}, s32[4]{0:T(128)}, u32[]{:S(2)}) copy-start(s32[4]{0:T(128)} %ranks_ref.1) | copy-start | bytes 52
  3.7 2.2 %collective-permute-start.4 = (bf16[16,128]{1,0:T(8,128)(2,1)S(1)}, bf16[16,128]{1,0:T(8,128)(2,1)S(1)}, u32[]{:S(2)}, u32[]{:S(2)}) collective-permute-start(bf16[16,128]{1,0:T(8,128)(2,1)S(1)} %coeffs.1), channel_id=1, source_target_pairs={{0,4},{1,5},{2,6},{3,7},{4,0},{5,1},{6,2},{7,3},{8,12},{9,13},{10,... | collective-permute-start | bytes 12296 | tf_op jit(solution)/shard_map/ppermute | solution.py:39
  3.8 8.7 %collective-permute-start = (bf16[4,16,512]{2,1,0:T(8,128)(2,1)S(1)}, bf16[4,16,512]{2,1,0:T(8,128)(2,1)S(1)}, u32[]{:S(2)}, u32[]{:S(2)}) collective-permute-start(bf16[4,16,512]{2,1,0:T(8,128)(2,1)S(1)} %copy-done.3), channel_id=1, source_target_pairs={{0,1},{1,0},{2,3},{3,2},{4,7},{5,6},{6,5},{7,4},{8,9},{9,8},{10,11... | collective-permute-start | bytes 196616 | tf_op jit(solution)/shard_map/ppermute | solution.py:39
  5.9 3.6 %collective-permute-start.5 = (bf16[1,16,128]{2,1,0:T(8,128)(2,1)S(1)}, bf16[1,16,128]{2,1,0:T(8,128)(2,1)S(1)}, u32[]{:S(2)}, u32[]{:S(2)}) collective-permute-start(bf16[1,16,128]{2,1,0:T(8,128)(2,1)S(1)} %add_bitcast_fusion), channel_id=1, source_target_pairs={{0,8},{1,9},{2,10},{3,11},{4,12},{5,13},{6,14},{7,15},{8,0},{9,1},... | collective-permute-start | bytes 12296 | tf_op jit(solution)/shard_map/ppermute | solution.py:39
  9.5 6.3 %collective-permute-start.6 = (bf16[2,16,128]{2,1,0:T(8,128)(2,1)S(1)}, bf16[2,16,128]{2,1,0:T(8,128)(2,1)S(1)}, u32[]{:S(2)}, u32[]{:S(2)}) collective-permute-start(bf16[2,16,128]{2,1,0:T(8,128)(2,1)S(1)} %pad_maximum_fusion.2), channel_id=1, source_target_pairs={{0,24},{1,25},{2,26},{3,27},{4,28},{5,29},{6,30},{7,31},{8,16},{9,... | collective-permute-start | bytes 24584 | tf_op jit(solution)/shard_map/ppermute | solution.py:39
  12.5 6.3 %collective-permute-start.1 = (bf16[8,16,512]{2,1,0:T(8,128)(2,1)S(1)}, bf16[8,16,512]{2,1,0:T(8,128)(2,1)S(1)}, u32[]{:S(2)}, u32[]{:S(2)}) collective-permute-start(bf16[8,16,512]{2,1,0:T(8,128)(2,1)S(1)} %constant_dynamic-update-slice_fusion.own_ref), channel_id=1, source_target_pairs={{0,3},{1,2},{2,1},{3,0},{4,5},{5,4},{6,7},{7,6},{8,11},{9,10},{10,... | collective-permute-start | bytes 393224 | tf_op jit(solution)/shard_map/ppermute | solution.py:39
  15.8 5.7 %collective-permute-start.7 = (bf16[4,16,128]{2,1,0:T(8,128)(2,1)S(1)}, bf16[4,16,128]{2,1,0:T(8,128)(2,1)S(1)}, u32[]{:S(2)}, u32[]{:S(2)}) collective-permute-start(bf16[4,16,128]{2,1,0:T(8,128)(2,1)S(1)} %pad_maximum_fusion.1), channel_id=1, source_target_pairs={{0,32},{1,33},{2,34},{3,35},{4,36},{5,37},{6,38},{7,39},{8,40},{9,... | collective-permute-start | bytes 49160 | tf_op jit(solution)/shard_map/ppermute | solution.py:39
  18.9 10.7 %collective-permute-start.2 = (bf16[8,16,512]{2,1,0:T(8,128)(2,1)S(1)}, bf16[8,16,512]{2,1,0:T(8,128)(2,1)S(1)}, u32[]{:S(2)}, u32[]{:S(2)}) collective-permute-start(bf16[8,16,512]{2,1,0:T(8,128)(2,1)S(1)} %get-tuple-element.6), channel_id=1, source_target_pairs={{0,4},{1,5},{2,6},{3,7},{4,0},{5,1},{6,2},{7,3},{8,12},{9,13},{10,... | collective-permute-start | bytes 393224 | tf_op jit(solution)/shard_map/ppermute | solution.py:39
  18.9 10.6 %collective-permute-start.3 = (bf16[8,16,512]{2,1,0:T(8,128)(2,1)S(1)}, bf16[8,16,512]{2,1,0:T(8,128)(2,1)S(1)}, u32[]{:S(2)}, u32[]{:S(2)}) collective-permute-start(bf16[8,16,512]{2,1,0:T(8,128)(2,1)S(1)} %get-tuple-element.7), channel_id=1, source_target_pairs={{0,124},{1,125},{2,126},{3,127},{4,8},{5,9},{6,10},{7,11},{8,4},{9... | collective-permute-start | bytes 393224 | tf_op jit(solution)/shard_map/ppermute | solution.py:39
  21.5 5.2 %collective-permute-start.8 = (bf16[8,16,128]{2,1,0:T(8,128)(2,1)S(1)}, bf16[8,16,128]{2,1,0:T(8,128)(2,1)S(1)}, u32[]{:S(2)}, u32[]{:S(2)}) collective-permute-start(bf16[8,16,128]{2,1,0:T(8,128)(2,1)S(1)} %pad_maximum_fusion.near_half_ref), channel_id=1, source_target_pairs={{0,96},{1,97},{2,98},{3,99},{4,100},{5,101},{6,102},{7,103},{8,104... | collective-permute-start | bytes 98312 | tf_op jit(solution)/shard_map/ppermute | solution.py:39
  26.7 1.2 %copy-start.2 = (bf16[16,16,2048]{2,1,0:T(8,128)(2,1)S(1)}, bf16[16,16,2048]{2,1,0:T(8,128)(2,1)}, u32[]{:S(2)}) copy-start(bf16[16,16,2048]{2,1,0:T(8,128)(2,1)} %param.16) | copy-start | bytes 3145732
  27.9 0.9 %copy-start.4 = (bf16[16,16,512]{2,1,0:T(8,128)(2,1)S(1)}, bf16[16,16,512]{2,1,0:T(8,128)(2,1)}, u32[]{:S(2)}) copy-start(bf16[16,16,512]{2,1,0:T(8,128)(2,1)} %param.13) | copy-start | bytes 786436
  29.6 3.4 %copy-start = (bf16[16,1,512,512]{3,2,1,0:T(8,128)(2,1)S(1)}, bf16[16,1,512,512]{3,2,1,0:T(8,128)(2,1)}, u32[]{:S(2)}) copy-start(bf16[16,1,512,512]{3,2,1,0:T(8,128)(2,1)} %param.11) | copy-start | bytes 25165828
  33.0 0.7 %copy-start.7 = (s32[16,1]{0,1:T(1,128)S(1)}, s32[16,1]{0,1:T(1,128)}, u32[]{:S(2)}) copy-start(s32[16,1]{0,1:T(1,128)} %param.12) | copy-start | bytes 196
  33.6 12.7 %copy-start.1 = (bf16[4,512,512]{2,1,0:T(8,128)(2,1)S(1)}, bf16[4,512,512]{2,1,0:T(8,128)(2,1)}, u32[]{:S(2)}) copy-start(bf16[4,512,512]{2,1,0:T(8,128)(2,1)} %inverse_ref.1) | copy-start | bytes 6291460
  33.6 12.7 %copy-start.5 = (f32[4,16,512]{2,1,0:T(8,128)S(1)}, f32[4,16,512]{2,1,0:T(8,128)}, u32[]{:S(2)}) copy-start(f32[4,16,512]{2,1,0:T(8,128)} %injected_ref.1) | copy-start | bytes 393220
  35.4 5.2 %collective-permute-start.9 = (bf16[8,16,512]{2,1,0:T(8,128)(2,1)S(1)}, bf16[8,16,512]{2,1,0:T(8,128)(2,1)S(1)}, u32[]{:S(2)}, u32[]{:S(2)}) collective-permute-start(bf16[8,16,512]{2,1,0:T(8,128)(2,1)S(1)} %near_sent.1), channel_id=1, source_target_pairs={{0,1},{1,0},{2,3},{3,2},{4,7},{5,6},{6,5},{7,4},{8,9},{9,8},{10,11... | collective-permute-start | bytes 393224 | tf_op jit(solution)/shard_map/ppermute | solution.py:39
  40.6 5.8 %collective-permute-start.10 = (bf16[4,16,512]{2,1,0:T(8,128)(2,1)S(1)}, bf16[4,16,512]{2,1,0:T(8,128)(2,1)S(1)}, u32[]{:S(2)}, u32[]{:S(2)}) collective-permute-start(bf16[4,16,512]{2,1,0:T(8,128)(2,1)S(1)} %fold.1), channel_id=1, source_target_pairs={{0,3},{1,2},{2,1},{3,0},{4,5},{5,4},{6,7},{7,6},{8,11},{9,10},{10,... | collective-permute-start | bytes 196616 | tf_op jit(solution)/shard_map/ppermute | solution.py:39

commit v2 on v1

v2 whole, which is shorter than its diff:
```python
import functools

import jax
import jax.numpy as jnp
from jax import lax
from jax.experimental import pallas as pl
from jax.experimental.pallas import tpu as pltpu
from jax.sharding import PartitionSpec as P


AXES = ("prod", "pre")
GRAY = (0, 1, 3, 2)
NT = (((1,), (1,)), ((), ()))
F32 = jnp.float32
BF16 = jnp.bfloat16


def pairs(rule):
    table = []
    for p in range(32):
        for a in range(4):
            q, b = rule(p, a)
            table.append((p * 4 + a, q * 4 + b))
    return table


def first_mask(p):
    return 1 if p % 2 == 0 else 3


CORE_SWAP = pairs(lambda p, a: (p ^ 1, a))
Y_SWAPS = tuple(pairs(lambda p, a, m=m: (p ^ (2 * m), a)) for m in (1, 3))
X_SWAPS = tuple(pairs(lambda p, a, m=m: (p ^ (8 * m), a)) for m in (1, 3))
Z_FIRST = pairs(lambda p, a: (p, a ^ first_mask(p)))
Z_SECOND = pairs(lambda p, a: (p, a ^ first_mask(p) ^ 2))
OTHER_CHIP = pairs(lambda p, a: (p, a ^ 1) if p in (0, 31) else (p + 1 if p % 2 else p - 1, a))


def send(x, table):
    return lax.ppermute(x, AXES, table)


def place():
    p = lax.axis_index("prod")
    a = lax.axis_index("pre")
    core = p & 1
    first = 1 + 2 * core
    second = 3 - 2 * core
    return p, a, core, first, second


def coeff_kernel(pot_hbm, basis_hbm, ranks_hbm, out_ref, room_ref, pot_ref, basis_ref, ranks_ref, sems):
    p = lax.axis_index("prod")
    copies = [
        pltpu.make_async_copy(pot_hbm, pot_ref, sems.at[0]),
        pltpu.make_async_copy(basis_hbm, basis_ref, sems.at[1]),
        pltpu.make_async_copy(ranks_hbm, ranks_ref, sems.at[2]),
    ]
    for copy in copies:
        copy.start()
    for copy in copies:
        copy.wait()
    pot = pot_ref[...].reshape(64, 512)
    basis = basis_ref[...].reshape(64, 512)
    both = jnp.concatenate([basis, basis], axis=0)
    full = lax.dot_general(pot, both, NT, preferred_element_type=F32)
    lane = lax.broadcasted_iota(jnp.int32, (16, 128), 1)
    here = (lane >> 6) == (p & 1)
    total = jnp.zeros((16, 128), F32)
    for j in range(4):
        keep = here & (((lane >> 4) & 3) == j) & ((lane & 15) < ranks_ref[j])
        total = total + jnp.where(keep, full[j * 16:(j + 1) * 16, :], 0.0)
    out_ref[...] = total.astype(BF16)


def join_kernel(mine_ref, theirs_ref, room_ref, out_ref):
    out_ref[0] = mine_ref[...] + theirs_ref[...]


def weights_kernel(near_half_ref, far_half_ref, couplings_ref, out_ref, sent_ref, gathered):
    p = lax.axis_index("prod")
    x = p >> 3
    y = (p >> 1) & 3
    for r in range(16):
        chip = (x ^ GRAY[r // 4]) * 4 + (y ^ GRAY[r % 4])
        piece = near_half_ref[r] if r < 8 else far_half_ref[r - 8]
        gathered[:, pl.ds(pl.multiple_of(chip * 128, 128), 128)] = piece
    weights = lax.dot_general(gathered[...], couplings_ref[...], NT, preferred_element_type=F32)
    out_ref[...] = weights
    sent_ref[...] = weights.astype(BF16)


def far_rows(piece, weights_ref, got_ref, row_ref):
    both = weights_ref[...] + got_ref[...].astype(F32)
    tall = jnp.concatenate([both] * 4, axis=0)
    row = lax.broadcasted_iota(jnp.int32, (64, 256), 0) >> 4
    col = lax.broadcasted_iota(jnp.int32, (64, 256), 1) >> 4
    spread = jnp.where(row + piece * 4 == col, tall, 0.0).astype(BF16)
    return jnp.dot(spread, row_ref[...], preferred_element_type=F32).reshape(4, 16, 512)


def select_kernel(own_ref, other_ref, group_ref, chip_ref, out_ref):
    _, a, core, first, second = place()
    for z in range(4):
        d = a ^ z
        slot = jnp.where(d == 0, 0, jnp.where(d == first, 1, jnp.where(d == second, 2, 3)))
        at = pl.multiple_of((slot & 1) * 4, 4)
        piece = jnp.where(slot < 2, own_ref[pl.ds(at, 4)], other_ref[pl.ds(at, 4)])
        group_ref[z * 4:(z + 1) * 4] = piece
        to_chip = (z < 2) == (core == 1) if False else ((z >> 1) ^ core) == 1

        @pl.when(to_chip)
        def _():
            chip_ref[(z & 1) * 4:(z & 1) * 4 + 4] = piece

        @pl.when(jnp.logical_not(to_chip))
        def _():
            out_ref[(z & 1) * 4:(z & 1) * 4 + 4] = piece


def near_kernel(keep, cols_ref, group_ref, chip_ref, outer_ref, near_ref, out_ref):
    p, a, core, first, second = place()
    base = p * 16
    for half in range(2):
        if keep:
            piece = a if half == 0 else a ^ second
        else:
            piece = a ^ first if half == 0 else a ^ 2
        for j in range(4):
            i = piece * 4 + j
            c = cols_ref[i] - base
            below = c < 0
            above = c >= 16
            halo = jnp.clip(jnp.where(below, c + 8, c - 16), 0, 7)
            from_chip = (below & (core == 1)) | (above & (core == 0))
            inside = jnp.logical_not(below | above)
            picked = jnp.where(from_chip, chip_ref[halo], outer_ref[halo])
            picked = jnp.where(inside, group_ref[jnp.clip(c, 0, 15)], picked)
            block = lax.dot_general(picked, near_ref[i], NT, preferred_element_type=F32)
            out_ref[half * 4 + j] = block.astype(out_ref.dtype)


def fold_kernel(kept_ref, got_ref, weights_ref, got_weights_ref, row_ref, out_ref):
    _, a, _, _, second = place()
    far = far_rows(a ^ second, weights_ref, got_weights_ref, row_ref)
    out_ref[...] = (kept_ref[4:8] + got_ref[4:8].astype(F32) + far).astype(BF16)


def own_kernel(kept_ref, got_ref, weights_ref, got_weights_ref, row_ref, injected_ref, out_ref):
    far = far_rows(lax.axis_index("pre"), weights_ref, got_weights_ref, row_ref)
    out_ref[...] = injected_ref[...] - (kept_ref[0:4] + got_ref[0:4].astype(F32) + far)


def final_kernel(own_ref, last_ref, inverse_ref, residual_ref, corrected_ref):
    for j in range(4):
        residual = own_ref[j] - last_ref[j].astype(F32)
        residual_ref[j] = residual
        corrected_ref[j] = lax.dot_general(
            residual.astype(BF16), inverse_ref[j], NT, preferred_element_type=F32
        )


VMEM = pl.BlockSpec(memory_space=pltpu.VMEM)
HBM = pl.BlockSpec(memory_space=pltpu.HBM)
SMEM = pl.BlockSpec(memory_space=pltpu.SMEM)


def call(kernel, out_shape, in_specs, scratch=(), flops=0, moved=0, limit=16 * 2**20, out_specs=None):
    many = isinstance(out_shape, (list, tuple))
    return pl.pallas_call(
        kernel,
        out_shape=out_shape,
        in_specs=in_specs,
        out_specs=out_specs or ([VMEM] * len(out_shape) if many else VMEM),
        scratch_shapes=list(scratch),
        compiler_params=pltpu.CompilerParams(vmem_limit_bytes=limit),
        cost_estimate=pl.CostEstimate(flops=flops, bytes_accessed=moved, transcendentals=0),
    )


def shape(dims, dtype):
    return jax.ShapeDtypeStruct(dims, dtype)


def compute(
    potentials,
    injected,
    near_blocks,
    near_cols,
    row_basis,
    col_basis,
    basis_ranks,
    couplings,
    inverses,
):
    first_z = send(potentials, Z_FIRST)
    coeffs, room = call(
        coeff_kernel, [pltpu.VMEM((16, 128), BF16), shape((20, 1024, 1024), BF16)], [HBM, HBM, HBM],
        scratch=[
            pltpu.VMEM((4, 16, 512), BF16), pltpu.VMEM((4, 16, 512), BF16), pltpu.SMEM((4,), jnp.int32),
            pltpu.SemaphoreType.DMA((3,)),
        ],
        moved=2**17, limit=63 * 2**20, out_specs=[VMEM, HBM],
    )(potentials, col_basis, basis_ranks)
    gathered = call(join_kernel, shape((1, 16, 128), BF16), [VMEM, VMEM, HBM], moved=2**25)(
        coeffs, send(coeffs, CORE_SWAP), room
    )
    for table in (Y_SWAPS[0], Y_SWAPS[1], X_SWAPS[0]):
        gathered = jnp.concatenate([gathered, send(gathered, table)], axis=0)
    others = send(gathered, X_SWAPS[1])
    own_pair = jnp.concatenate([potentials, first_z], axis=0)
    second_z = send(own_pair, Z_SECOND)
    group, to_chip, to_outer = call(
        select_kernel,
        [shape((16, 16, 512), BF16), shape((8, 16, 512), BF16), shape((8, 16, 512), BF16)],
        [VMEM, VMEM], moved=2**19,
    )(own_pair, second_z)
    outer = send(to_outer, OTHER_CHIP)
    chip = send(to_chip, CORE_SWAP)
    blocks = near_blocks.reshape(16, 512, 512)
    cols = near_cols.reshape(16)
    near_specs = [SMEM] + [VMEM] * 4
    sent = call(
        functools.partial(near_kernel, False), shape((8, 16, 512), BF16), near_specs,
        moved=2**22, flops=2**26,
    )(cols, group, chip, outer, blocks)
    got = send(sent, Z_FIRST)
    weights, sent_weights = call(
        weights_kernel, [shape((16, 256), F32), shape((16, 256), BF16)], [VMEM] * 3,
        scratch=[pltpu.VMEM((16, 2048), BF16)], moved=2**20, flops=2**24,
    )(gathered, others, couplings.reshape(256, 2048))
    got_weights = send(sent_weights, Z_FIRST)
    kept = call(
        functools.partial(near_kernel, True), shape((8, 16, 512), F32), near_specs,
        moved=2**22, flops=2**26,
    )(cols, group, chip, outer, blocks)
    rows = row_basis.reshape(256, 512)
    folded = call(fold_kernel, shape((4, 16, 512), BF16), [VMEM] * 5, moved=2**18)(
        kept, got, weights, got_weights, rows
    )
    last = send(folded, Z_SECOND)
    own = call(own_kernel, shape((4, 16, 512), F32), [VMEM] * 6, moved=2**18)(
        kept, got, weights, got_weights, rows, injected
    )
    return call(
        final_kernel, [shape((4, 16, 512), F32), shape((4, 16, 512), F32)], [VMEM] * 3,
        moved=2**21, flops=2**25,
    )(own, last, inverses)


def solution(mesh):
    return jax.shard_map(
        compute,
        mesh=mesh,
        in_specs=(
            P(("prod", "pre"), None, None),
            P(("prod", "pre"), None, None),
            P("prod", "pre", None, None),
            P("prod", "pre"),
            P("prod", None, None),
            P(("prod", "pre"), None, None),
            P(("prod", "pre")),
            P("prod", None, "pre"),
            P(("prod", "pre"), None, None),
        ),
        out_specs=(P(("prod", "pre"), None, None), P(("prod", "pre"), None, None)),
        check_vma=False,
    )
```

time: 48 us -> 41 us (0.85)
  local copies, waits for them, and re-layouts: 8.55 us -> 0.92 us
  starting transfers between devices: 19 us -> 20.9 us
  waiting for transfers between devices: 13 us -> 11.5 us
    unnamed x19 -> x13, local copies, waits for them, and re-layouts: 8.54 us -> 0.91 us
    ppermute x11 -> x12, starting transfers between devices: 19 us -> 20.9 us  [send(): return lax.ppermute(x, AXES, table)]
    ppermute x11 -> x12, waiting for transfers between devices: 13 us -> 11.5 us  [send(): return lax.ppermute(x, AXES, table)]
    pallas_call x7 -> x9, Pallas kernels: 6.29 us -> 6.65 us  [the longest x1 1.74 us: compute(): call(functools.partial(near_kernel, False), shape((8, 16, 512), BF16), ne...]
  transfers between devices with their start and end apart: 11 -> 12, of which waited for: 5 -> 7; matrix products, arithmetic and copies ran while one was open for 0% -> 2% of each run, Pallas kernels for 5% -> 13%
where the time goes in v2:
time: 41 us; the launch traced here: 40.7 us
  starting transfers between devices  20.9 us (51%)
  waiting for transfers between devices  11.5 us (28%)
  Pallas kernels  6.65 us (16%)
  local copies, waits for them, and re-layouts  0.92 us (2%)
  between operations  0.74 us (2%)
    ppermute x12, starting transfers between devices, send(): return lax.ppermute(x, AXES, table)  20.9 us
    ppermute x12, waiting for transfers between devices, send(): return lax.ppermute(x, AXES, table)  11.5 us
    pallas_call x1, Pallas kernels, compute(): call(functools.partial(near_kernel, False), shape((8, 16, 512), BF16), ne...  1.74 us
    pallas_call x1, Pallas kernels, compute(): call(functools.partial(near_kernel, True), shape((8, 16, 512), F32), near...  1.74 us
    pallas_call x1, Pallas kernels, compute(): call(final_kernel, [shape((4, 16, 512), F32), shape((4, 16, 512), F32)],...  1.32 us
    pallas_call x1, Pallas kernels, compute(): call(coeff_kernel, [pltpu.VMEM((16, 128), BF16), shape((20, 1024, 1024),...  1.07 us
    unnamed x13, local copies, waits for them, and re-layouts  0.91 us
  transfers between devices with their start and end apart: 12, of which 7 were waited for; matrix products, arithmetic and copies ran while one was open for 2% of the time, Pallas kernels for 13%

profile of v2, /device:TPU:0, one launch (start us, length us, event | category | flops | bytes accessed | tf_op | source)
XLA Modules:
  0.0 40.7 jit_solution(2894040762398232744)
XLA Ops:
  0.6 2.1 %collective-permute-start = (bf16[4,16,512]{2,1,0:T(8,128)(2,1)}, bf16[4,16,512]{2,1,0:T(8,128)(2,1)S(1)}, u32[]{:S(2)}, u32[]{:S(2)}) collective-permute-start(bf16[4,16,512]{2,1,0:T(8,128)(2,1)} %pot_hbm.1), channel_id=1, source_target_pairs={{0,1},{1,0},{2,3},{3,2},{4,7},{5,6},{6,5},{7,4},{8,9},{9,8},{10,11... | collective-permute-start | bytes 196616 | tf_op jit(solution)/shard_map/ppermute | solution.py:40
  2.7 0.9 %constant_dynamic-update-slice_fusion.1 = bf16[8,16,512]{2,1,0:T(8,128)(2,1)S(1)} fusion(bf16[4,16,512]{2,1,0:T(8,128)(2,1)} %pot_hbm.1), kind=kLoop, calls=%fused_computation.4 | loop fusion | bytes 131072
  3.6 1.6 %collective-permute-done = bf16[4,16,512]{2,1,0:T(8,128)(2,1)S(1)} collective-permute-done((bf16[4,16,512]{2,1,0:T(8,128)(2,1)}, bf16[4,16,512]{2,1,0:T(8,128)(2,1)S(1)}, u32[]{:S(2)}, u32[]{:S(2)}) %collective-permute-start) | collective-permute-done | bytes 65568 | tf_op jit(solution)/shard_map/ppermute | solution.py:40
  5.2 4.1 %collective-permute-start.1 = (bf16[8,16,512]{2,1,0:T(8,128)(2,1)S(1)}, bf16[8,16,512]{2,1,0:T(8,128)(2,1)S(1)}, u32[]{:S(2)}, u32[]{:S(2)}) collective-permute-start(bf16[8,16,512]{2,1,0:T(8,128)(2,1)S(1)} %constant_dynamic-update-slice_fusion.own_ref), channel_id=1, source_target_pairs={{0,3},{1,2},{2,1},{3,0},{4,5},{5,4},{6,7},{7,6},{8,11},{9,10},{10,... | collective-permute-start | bytes 393224 | tf_op jit(solution)/shard_map/ppermute | solution.py:40
  9.3 1.1 %shard_map.107 = (bf16[16,128]{1,0:T(8,128)(2,1)S(1)}, bf16[20,1024,1024]{2,1,0:T(8,128)(2,1)}) custom-call(bf16[4,16,512]{2,1,0:T(8,128)(2,1)} %pot_hbm.1, bf16[4,16,512]{2,1,0:T(8,128)(2,1)} %basis_hbm.1, s32[4]{0:T(128)} %ranks_hbm.1), custom_call_target="tpu_custom_call" | custom-call | bytes 131072 | tf_op jit(solution)/shard_map/pallas_call | solution.py:197
  10.4 0.1 collective-permute-start.5
  10.5 1.2 %collective-permute-done.5.theirs_ref = bf16[16,128]{1,0:T(8,128)(2,1)S(1)} collective-permute-done((bf16[16,128]{1,0:T(8,128)(2,1)S(1)}, bf16[16,128]{1,0:T(8,128)(2,1)S(1)}, u32[]{:S(2)}, u32[]{:S(2)}) %collective-permute-start.5) | collective-permute-done | bytes 4128 | tf_op jit(solution)/shard_map/ppermute | solution.py:40
  11.7 0.0 copy-start
  11.7 0.0 copy-start.5
  11.7 0.0 copy-start.3
  11.7 1.7 %collective-permute-start.6 = (bf16[1,16,128]{2,1,0:T(8,128)(2,1)S(1)}, bf16[1,16,128]{2,1,0:T(8,128)(2,1)S(1)}, u32[]{:S(2)}, u32[]{:S(2)}) collective-permute-start(bf16[1,16,128]{2,1,0:T(8,128)(2,1)S(1)} %shard_map.108), channel_id=1, source_target_pairs={{0,8},{1,9},{2,10},{3,11},{4,12},{5,13},{6,14},{7,15},{8,0},{9,1},... | collective-permute-start | bytes 12296 | tf_op jit(solution)/shard_map/ppermute | solution.py:40
  13.3 0.0 collective-permute-done.1.other_ref
  13.3 0.1 shard_map.104
  13.4 0.1 collective-permute-start.2
  13.5 0.1 collective-permute-start.3
  13.6 1.8 %collective-permute-done.6 = bf16[1,16,128]{2,1,0:T(8,128)(2,1)S(1)} collective-permute-done((bf16[1,16,128]{2,1,0:T(8,128)(2,1)S(1)}, bf16[1,16,128]{2,1,0:T(8,128)(2,1)S(1)}, u32[]{:S(2)}, u32[]{:S(2)}) %collective-permute-start.6) | collective-permute-done | bytes 4128 | tf_op jit(solution)/shard_map/ppermute | solution.py:40
  15.4 3.0 %collective-permute-start.7 = (bf16[2,16,128]{2,1,0:T(8,128)(2,1)S(1)}, bf16[2,16,128]{2,1,0:T(8,128)(2,1)S(1)}, u32[]{:S(2)}, u32[]{:S(2)}) collective-permute-start(bf16[2,16,128]{2,1,0:T(8,128)(2,1)S(1)} %pad_maximum_fusion.2), channel_id=1, source_target_pairs={{0,24},{1,25},{2,26},{3,27},{4,28},{5,29},{6,30},{7,31},{8,16},{9,... | collective-permute-start | bytes 24584 | tf_op jit(solution)/shard_map/ppermute | solution.py:40
  18.4 1.8 %collective-permute-done.7 = bf16[2,16,128]{2,1,0:T(8,128)(2,1)S(1)} collective-permute-done((bf16[2,16,128]{2,1,0:T(8,128)(2,1)S(1)}, bf16[2,16,128]{2,1,0:T(8,128)(2,1)S(1)}, u32[]{:S(2)}, u32[]{:S(2)}) %collective-permute-start.7) | collective-permute-done | bytes 8224 | tf_op jit(solution)/shard_map/ppermute | solution.py:40
  20.2 1.9 %collective-permute-start.8 = (bf16[4,16,128]{2,1,0:T(8,128)(2,1)S(1)}, bf16[4,16,128]{2,1,0:T(8,128)(2,1)S(1)}, u32[]{:S(2)}, u32[]{:S(2)}) collective-permute-start(bf16[4,16,128]{2,1,0:T(8,128)(2,1)S(1)} %pad_maximum_fusion.1), channel_id=1, source_target_pairs={{0,32},{1,33},{2,34},{3,35},{4,36},{5,37},{6,38},{7,39},{8,40},{9,... | collective-permute-start | bytes 49160 | tf_op jit(solution)/shard_map/ppermute | solution.py:40
  22.1 0.0 collective-permute-done.2.chip_ref
  22.1 0.0 collective-permute-done.3.outer_ref
  22.1 0.0 copy-done
  22.2 0.0 copy-done.5
  22.2 0.0 copy-start.2
  22.2 0.0 copy-start.4
  22.2 0.0 copy-start.1
  22.2 1.7 %shard_map.106 = bf16[8,16,512]{2,1,0:T(8,128)(2,1)S(1)} custom-call(s32[16]{0:T(128)S(1)} %bitcast.9, bf16[16,16,512]{2,1,0:T(8,128)(2,1)S(1)} %get-tuple-element.9.group_ref, bf16[8,16,512]{2,1,0:T(8,128)(2,1)S(1)} %collective-permute-done.2.chip_ref, bf16[8,16,512]{2,1,0:T(8,128)(2,1)S(1)} %collective-permute-done.3.outer_ref, ...), custom_call_target="tpu_custom_call" | custom-call | flops 67108864 | bytes 4194304 | tf_op jit(solution)/shard_map/pallas_call | solution.py:223
  23.9 0.0 collective-permute-start.4
  23.9 0.0 collective-permute-done.8
  24.0 3.4 %collective-permute-start.9 = (bf16[8,16,128]{2,1,0:T(8,128)(2,1)S(1)}, bf16[8,16,128]{2,1,0:T(8,128)(2,1)S(1)}, u32[]{:S(2)}, u32[]{:S(2)}) collective-permute-start(bf16[8,16,128]{2,1,0:T(8,128)(2,1)S(1)} %pad_maximum_fusion.near_half_ref), channel_id=1, source_target_pairs={{0,96},{1,97},{2,98},{3,99},{4,100},{5,101},{6,102},{7,103},{8,104... | collective-permute-start | bytes 98312 | tf_op jit(solution)/shard_map/ppermute | solution.py:40
  27.4 2.2 %collective-permute-done.9.far_half_ref = bf16[8,16,128]{2,1,0:T(8,128)(2,1)S(1)} collective-permute-done((bf16[8,16,128]{2,1,0:T(8,128)(2,1)S(1)}, bf16[8,16,128]{2,1,0:T(8,128)(2,1)S(1)}, u32[]{:S(2)}, u32[]{:S(2)}) %collective-permute-start.9) | collective-permute-done | bytes 32800 | tf_op jit(solution)/shard_map/ppermute | solution.py:40
  29.6 0.0 copy-done.3
  29.6 0.4 shard_map.109
  30.0 1.6 %collective-permute-start.10 = (bf16[16,256]{1,0:T(8,128)(2,1)S(1)}, bf16[16,256]{1,0:T(8,128)(2,1)S(1)}, u32[]{:S(2)}, u32[]{:S(2)}) collective-permute-start(bf16[16,256]{1,0:T(8,128)(2,1)S(1)} %get-tuple-element.15), channel_id=1, source_target_pairs={{0,1},{1,0},{2,3},{3,2},{4,7},{5,6},{6,5},{7,4},{8,9},{9,8},{10,11... | collective-permute-start | bytes 24584 | tf_op jit(solution)/shard_map/ppermute | solution.py:40
  31.6 1.7 %shard_map.105.kept_ref = f32[8,16,512]{2,1,0:T(8,128)S(1)} custom-call(s32[16]{0:T(128)S(1)} %bitcast.10, bf16[16,16,512]{2,1,0:T(8,128)(2,1)S(1)} %get-tuple-element.9.group_ref, bf16[8,16,512]{2,1,0:T(8,128)(2,1)S(1)} %collective-permute-done.2.chip_ref, bf16[8,16,512]{2,1,0:T(8,128)(2,1)S(1)} %collective-permute-done.3.outer_ref, ...), custom_call_target="tpu_custom_call" | custom-call | flops 67108864 | bytes 4194304 | tf_op jit(solution)/shard_map/pallas_call | solution.py:233
  33.3 0.3 collective-permute-done.10.got_weights_ref
  33.7 0.0 collective-permute-done.4.got_ref
  33.7 0.0 copy-done.2
  33.7 0.2 shard_map.111
  33.9 2.8 %collective-permute-start.11 = (bf16[4,16,512]{2,1,0:T(8,128)(2,1)S(1)}, bf16[4,16,512]{2,1,0:T(8,128)(2,1)S(1)}, u32[]{:S(2)}, u32[]{:S(2)}) collective-permute-start(bf16[4,16,512]{2,1,0:T(8,128)(2,1)S(1)} %shard_map.111), channel_id=1, source_target_pairs={{0,3},{1,2},{2,1},{3,0},{4,5},{5,4},{6,7},{7,6},{8,11},{9,10},{10,... | collective-permute-start | bytes 196616 | tf_op jit(solution)/shard_map/ppermute | solution.py:40
  36.6 0.0 copy-done.4
  36.6 0.2 shard_map.110.own_ref
  36.8 2.6 %collective-permute-done.11.last_ref = bf16[4,16,512]{2,1,0:T(8,128)(2,1)S(1)} collective-permute-done((bf16[4,16,512]{2,1,0:T(8,128)(2,1)S(1)}, bf16[4,16,512]{2,1,0:T(8,128)(2,1)S(1)}, u32[]{:S(2)}, u32[]{:S(2)}) %collective-permute-start.11) | collective-permute-done | bytes 65568 | tf_op jit(solution)/shard_map/ppermute | solution.py:40
  39.4 0.0 copy-done.1
  39.4 1.3 %shard_map.112 = (f32[4,16,512]{2,1,0:T(8,128)}, f32[4,16,512]{2,1,0:T(8,128)}) custom-call(f32[4,16,512]{2,1,0:T(8,128)S(1)} %shard_map.110.own_ref, bf16[4,16,512]{2,1,0:T(8,128)(2,1)S(1)} %collective-permute-done.11.last_ref, bf16[4,512,512]{2,1,0:T(8,128)(2,1)S(1)} %copy-done.1), custom_call_target="tpu_custom_call" | custom-call | flops 33554432 | bytes 2097152 | tf_op jit(solution)/shard_map/pallas_call | solution.py:245
  (5 shorter events, 0.0 us)
Async XLA Ops:
  0.6 4.6 %collective-permute-start = (bf16[4,16,512]{2,1,0:T(8,128)(2,1)}, bf16[4,16,512]{2,1,0:T(8,128)(2,1)S(1)}, u32[]{:S(2)}, u32[]{:S(2)}) collective-permute-start(bf16[4,16,512]{2,1,0:T(8,128)(2,1)} %pot_hbm.1), channel_id=1, source_target_pairs={{0,1},{1,0},{2,3},{3,2},{4,7},{5,6},{6,5},{7,4},{8,9},{9,8},{10,11... | collective-permute-start | bytes 196616 | tf_op jit(solution)/shard_map/ppermute | solution.py:40
  5.2 8.1 %collective-permute-start.1 = (bf16[8,16,512]{2,1,0:T(8,128)(2,1)S(1)}, bf16[8,16,512]{2,1,0:T(8,128)(2,1)S(1)}, u32[]{:S(2)}, u32[]{:S(2)}) collective-permute-start(bf16[8,16,512]{2,1,0:T(8,128)(2,1)S(1)} %constant_dynamic-update-slice_fusion.own_ref), channel_id=1, source_target_pairs={{0,3},{1,2},{2,1},{3,0},{4,5},{5,4},{6,7},{7,6},{8,11},{9,10},{10,... | collective-permute-start | bytes 393224 | tf_op jit(solution)/shard_map/ppermute | solution.py:40
  10.4 1.2 %collective-permute-start.5 = (bf16[16,128]{1,0:T(8,128)(2,1)S(1)}, bf16[16,128]{1,0:T(8,128)(2,1)S(1)}, u32[]{:S(2)}, u32[]{:S(2)}) collective-permute-start(bf16[16,128]{1,0:T(8,128)(2,1)S(1)} %get-tuple-element.12.mine_ref), channel_id=1, source_target_pairs={{0,4},{1,5},{2,6},{3,7},{4,0},{5,1},{6,2},{7,3},{8,12},{9,13},{10,... | collective-permute-start | bytes 12296 | tf_op jit(solution)/shard_map/ppermute | solution.py:40
  11.7 10.5 %copy-start = (bf16[16,1,512,512]{3,2,1,0:T(8,128)(2,1)S(1)}, bf16[16,1,512,512]{3,2,1,0:T(8,128)(2,1)}, u32[]{:S(2)}) copy-start(bf16[16,1,512,512]{3,2,1,0:T(8,128)(2,1)} %param.11) | copy-start | bytes 25165828
  11.7 10.5 %copy-start.5 = (s32[16,1]{0,1:T(1,128)S(1)}, s32[16,1]{0,1:T(1,128)}, u32[]{:S(2)}) copy-start(s32[16,1]{0,1:T(1,128)} %param.12) | copy-start | bytes 196
  11.7 18.0 %copy-start.3 = (bf16[16,16,2048]{2,1,0:T(8,128)(2,1)S(1)}, bf16[16,16,2048]{2,1,0:T(8,128)(2,1)}, u32[]{:S(2)}) copy-start(bf16[16,16,2048]{2,1,0:T(8,128)(2,1)} %param.16) | copy-start | bytes 3145732
  11.7 3.7 %collective-permute-start.6 = (bf16[1,16,128]{2,1,0:T(8,128)(2,1)S(1)}, bf16[1,16,128]{2,1,0:T(8,128)(2,1)S(1)}, u32[]{:S(2)}, u32[]{:S(2)}) collective-permute-start(bf16[1,16,128]{2,1,0:T(8,128)(2,1)S(1)} %shard_map.108), channel_id=1, source_target_pairs={{0,8},{1,9},{2,10},{3,11},{4,12},{5,13},{6,14},{7,15},{8,0},{9,1},... | collective-permute-start | bytes 12296 | tf_op jit(solution)/shard_map/ppermute | solution.py:40
  13.4 8.7 %collective-permute-start.2 = (bf16[8,16,512]{2,1,0:T(8,128)(2,1)S(1)}, bf16[8,16,512]{2,1,0:T(8,128)(2,1)S(1)}, u32[]{:S(2)}, u32[]{:S(2)}) collective-permute-start(bf16[8,16,512]{2,1,0:T(8,128)(2,1)S(1)} %get-tuple-element.10), channel_id=1, source_target_pairs={{0,4},{1,5},{2,6},{3,7},{4,0},{5,1},{6,2},{7,3},{8,12},{9,13},{10,... | collective-permute-start | bytes 393224 | tf_op jit(solution)/shard_map/ppermute | solution.py:40
  13.5 8.6 %collective-permute-start.3 = (bf16[8,16,512]{2,1,0:T(8,128)(2,1)S(1)}, bf16[8,16,512]{2,1,0:T(8,128)(2,1)S(1)}, u32[]{:S(2)}, u32[]{:S(2)}) collective-permute-start(bf16[8,16,512]{2,1,0:T(8,128)(2,1)S(1)} %get-tuple-element.11), channel_id=1, source_target_pairs={{0,1},{1,0},{2,3},{3,2},{4,8},{5,9},{6,10},{7,11},{8,4},{9,5},{10,... | collective-permute-start | bytes 393224 | tf_op jit(solution)/shard_map/ppermute | solution.py:40
  15.4 4.9 %collective-permute-start.7 = (bf16[2,16,128]{2,1,0:T(8,128)(2,1)S(1)}, bf16[2,16,128]{2,1,0:T(8,128)(2,1)S(1)}, u32[]{:S(2)}, u32[]{:S(2)}) collective-permute-start(bf16[2,16,128]{2,1,0:T(8,128)(2,1)S(1)} %pad_maximum_fusion.2), channel_id=1, source_target_pairs={{0,24},{1,25},{2,26},{3,27},{4,28},{5,29},{6,30},{7,31},{8,16},{9,... | collective-permute-start | bytes 24584 | tf_op jit(solution)/shard_map/ppermute | solution.py:40
  20.2 3.7 %collective-permute-start.8 = (bf16[4,16,128]{2,1,0:T(8,128)(2,1)S(1)}, bf16[4,16,128]{2,1,0:T(8,128)(2,1)S(1)}, u32[]{:S(2)}, u32[]{:S(2)}) collective-permute-start(bf16[4,16,128]{2,1,0:T(8,128)(2,1)S(1)} %pad_maximum_fusion.1), channel_id=1, source_target_pairs={{0,32},{1,33},{2,34},{3,35},{4,36},{5,37},{6,38},{7,39},{8,40},{9,... | collective-permute-start | bytes 49160 | tf_op jit(solution)/shard_map/ppermute | solution.py:40
  22.2 11.5 %copy-start.2 = (bf16[16,16,512]{2,1,0:T(8,128)(2,1)S(1)}, bf16[16,16,512]{2,1,0:T(8,128)(2,1)}, u32[]{:S(2)}) copy-start(bf16[16,16,512]{2,1,0:T(8,128)(2,1)} %param.13) | copy-start | bytes 786436
  22.2 14.5 %copy-start.4 = (f32[4,16,512]{2,1,0:T(8,128)S(1)}, f32[4,16,512]{2,1,0:T(8,128)}, u32[]{:S(2)}) copy-start(f32[4,16,512]{2,1,0:T(8,128)} %injected_ref.1) | copy-start | bytes 393220
  22.2 17.2 %copy-start.1 = (bf16[4,512,512]{2,1,0:T(8,128)(2,1)S(1)}, bf16[4,512,512]{2,1,0:T(8,128)(2,1)}, u32[]{:S(2)}) copy-start(bf16[4,512,512]{2,1,0:T(8,128)(2,1)} %inverse_ref.1) | copy-start | bytes 6291460
  23.9 9.7 %collective-permute-start.4 = (bf16[8,16,512]{2,1,0:T(8,128)(2,1)S(1)}, bf16[8,16,512]{2,1,0:T(8,128)(2,1)S(1)}, u32[]{:S(2)}, u32[]{:S(2)}) collective-permute-start(bf16[8,16,512]{2,1,0:T(8,128)(2,1)S(1)} %shard_map.106), channel_id=1, source_target_pairs={{0,1},{1,0},{2,3},{3,2},{4,7},{5,6},{6,5},{7,4},{8,9},{9,8},{10,11... | collective-permute-start | bytes 393224 | tf_op jit(solution)/shard_map/ppermute | solution.py:40
  24.0 5.6 %collective-permute-start.9 = (bf16[8,16,128]{2,1,0:T(8,128)(2,1)S(1)}, bf16[8,16,128]{2,1,0:T(8,128)(2,1)S(1)}, u32[]{:S(2)}, u32[]{:S(2)}) collective-permute-start(bf16[8,16,128]{2,1,0:T(8,128)(2,1)S(1)} %pad_maximum_fusion.near_half_ref), channel_id=1, source_target_pairs={{0,96},{1,97},{2,98},{3,99},{4,100},{5,101},{6,102},{7,103},{8,104... | collective-permute-start | bytes 98312 | tf_op jit(solution)/shard_map/ppermute | solution.py:40
  30.0 3.7 %collective-permute-start.10 = (bf16[16,256]{1,0:T(8,128)(2,1)S(1)}, bf16[16,256]{1,0:T(8,128)(2,1)S(1)}, u32[]{:S(2)}, u32[]{:S(2)}) collective-permute-start(bf16[16,256]{1,0:T(8,128)(2,1)S(1)} %get-tuple-element.15), channel_id=1, source_target_pairs={{0,1},{1,0},{2,3},{3,2},{4,7},{5,6},{6,5},{7,4},{8,9},{9,8},{10,11... | collective-permute-start | bytes 24584 | tf_op jit(solution)/shard_map/ppermute | solution.py:40
  33.9 5.6 %collective-permute-start.11 = (bf16[4,16,512]{2,1,0:T(8,128)(2,1)S(1)}, bf16[4,16,512]{2,1,0:T(8,128)(2,1)S(1)}, u32[]{:S(2)}, u32[]{:S(2)}) collective-permute-start(bf16[4,16,512]{2,1,0:T(8,128)(2,1)S(1)} %shard_map.111), channel_id=1, source_target_pairs={{0,3},{1,2},{2,1},{3,0},{4,5},{5,4},{6,7},{7,6},{8,11},{9,10},{10,... | collective-permute-start | bytes 196616 | tf_op jit(solution)/shard_map/ppermute | solution.py:40
